TPU v7x, 256 devices: a whole 4x4x8 slice. The times are simulated.
256 devices in a mesh: dp: 32 (over z, x), mp: 8 (over y, core).
Axes of the slice: x: 4, y: 4, z: 8, core: 2. Of those that a mesh axis runs over, the one named last changes fastest.
Arguments:
- tokens: bfloat16 [32768, 8192], P('dp', 'mp'), may hold values from -6 to 6
- value_weight: bfloat16 [8192, 1024], P('mp'), may hold values from -0.0625 to 0.0625
- adapter_down_panels: bfloat16 [96, 64, 8192], P('dp', None, 'mp'), may hold values from -0.0625 to 0.0625
- adapter_up_panels: bfloat16 [96, 64, 1024], P('dp', None, 'mp'), may hold values from -0.75 to 0.75
- cotangent: bfloat16 [32768, 1024], P('dp', 'mp'), may hold values from -6 to 6
- block_list_entry: int32 [1024], P('dp'), may hold values from 0 to 31, as said below
- device_tenant_list: int32 [1024], P('dp'), may hold values from 0 to 95, as said below
- tenant_location_map: int32 [96], replicated, may hold values from 0 to 95, as said below
Outputs:
- values: bfloat16 [32768, 1024], P('dp', 'mp')
- token_gradient: bfloat16 [32768, 8192], P('dp', 'mp')
- grad_a: bfloat16 [96, 64, 8192], P('dp', None, 'mp')
- grad_b: bfloat16 [96, 64, 1024], P('dp', None, 'mp')
Inputs may be any that keep to these rules, and one draw needn't show every extreme that they name: `device_tenant_list`: each entry names a tenant; no tenant stands twice in one list. Of one device's 32 entries, at most 2 name tenants whose storage location tenant_location_map[t] lies on one dp index (tenant_location_map[t] // 3), and every device's list has 2 entries on some one dp index. A permutation: tenant t's panels are row tenant_location_map[t] of adapter_down_panels and adapter_up_panels. `block_list_entry`: every entry of a device's tenant list is named by at least one of that device's row blocks.
All inputs are finite; a program needn't handle non-finite values.
Results may differ from a plain program's by a relative error of at most 0.0057.
Values may be sent and summed in bfloat16 or wider, within the bound.
A program may use at most 128 MiB of HBM per device.

v0:
```python
import jax
import jax.numpy as jnp
import numpy as np
from jax import lax
from jax.sharding import Mesh
from jax.sharding import PartitionSpec as P

MOST = 2
DP = ("dz", "dx")


def earlier_same(group):
    count = group.shape[-1]
    ids = jnp.arange(count, dtype=jnp.int32)
    same = (group[..., :, None] == group[..., None, :]) & (ids[:, None] > ids[None, :])
    return jnp.sum(same.astype(jnp.int32), axis=-1)


def shards(
    tokens,
    value_weight,
    adapter_down_panels,
    adapter_up_panels,
    cotangent,
    block_list_entry,
    device_tenant_list,
    tenant_location_map,
):
    rows, width_loc = tokens.shape
    stored, rank, _ = adapter_down_panels.shape
    out_loc = adapter_up_panels.shape[2]
    blocks = block_list_entry.shape[0]
    blk = rows // blocks
    n_z = lax.axis_size("dz")
    n_x = lax.axis_size("dx")
    per_x = min(MOST * n_z, blocks)
    capacity = n_x * per_x
    my_x = lax.axis_index("dx")
    column = n_z * stored
    tenant = jnp.take(device_tenant_list, block_list_entry, mode="clip")
    location = jnp.take(tenant_location_map, tenant, mode="clip")
    owner_x = location // stored % n_x
    position = jnp.clip(owner_x * per_x + earlier_same(owner_x), 0, capacity - 1)
    slot_ids = jnp.arange(capacity, dtype=jnp.int32)
    block_ids = jnp.arange(blocks, dtype=jnp.int32)
    source = jnp.sum(
        jnp.where(position[None, :] == slot_ids[:, None], block_ids[None, :], 0), axis=1
    )
    base_part = lax.dot_general(
        value_weight, tokens, (((0,), (1,)), ((), ())), preferred_element_type=jnp.float32
    )
    location_tied, base_part = lax.optimization_barrier((location, base_part))
    base_t = lax.psum_scatter(base_part, "mp", scatter_dimension=0, tiled=True)
    x_location = lax.all_gather(location_tied, "dx", axis=0, tiled=False)
    x_owner_x = x_location // stored % n_x
    x_rank = earlier_same(x_owner_x)
    in_column = x_location // stored // n_x * stored + x_location % stored
    mine = x_owner_x == my_x
    slot_panel = (
        jnp.stack(
            [
                jnp.sum(jnp.where(mine & (x_rank == c), in_column + 1, 0), axis=1)
                for c in range(per_x)
            ],
            axis=1,
        ).reshape(capacity)
        - 1
    )
    panel_ids = jnp.arange(column, dtype=jnp.int32)
    slot_of = x_rank + (jnp.arange(n_x, dtype=jnp.int32) * per_x)[:, None]
    panel_slot = (
        jnp.sum(
            jnp.where(
                mine[None, :, :] & (in_column[None, :, :] == panel_ids[:, None, None]),
                slot_of[None, :, :] + 1,
                0,
            ),
            axis=2,
        )
        - 1
    )
    panel_used = panel_slot >= 0
    panel_slot = jnp.clip(panel_slot, 0, capacity - 1)
    both_col = lax.all_gather(
        jnp.concatenate([adapter_down_panels, adapter_up_panels], axis=2), "dz", axis=0, tiled=True
    )
    down_col = both_col[:, :, :width_loc]
    up_col = both_col[:, :, width_loc:]
    n_mp = lax.axis_size("mp")
    token_blocks = tokens.reshape(blocks, blk, width_loc)
    cot_blocks = cotangent.reshape(blocks, blk, out_loc)
    send = jnp.concatenate(
        [
            jnp.take(token_blocks, source, axis=0, mode="clip"),
            jnp.take(cot_blocks, source, axis=0, mode="clip"),
        ],
        axis=2,
    )
    recv = lax.all_to_all(send, "dx", split_axis=0, concat_axis=0, tiled=True)
    tok_recv = recv[:, :, :width_loc]
    cot_recv = recv[:, :, width_loc:]
    panel_at = jnp.clip(slot_panel, 0, column - 1)
    down_sel = jnp.take(down_col, panel_at, axis=0, mode="clip")
    up_sel = jnp.take(up_col, panel_at, axis=0, mode="clip")
    down_part = jnp.einsum("snd,srd->snr", tok_recv, down_sel, preferred_element_type=jnp.float32)
    up_part = jnp.einsum("snc,src->snr", cot_recv, up_sel, preferred_element_type=jnp.float32)
    both = lax.psum(jnp.stack([down_part, up_part]), "mp").astype(jnp.bfloat16)
    cot_parts = lax.all_gather(cotangent, "mp", axis=0, tiled=False)
    down_low = both[0]
    up_grad = both[1]
    adapter_out = jnp.einsum("snr,src->snc", down_low, up_sel, preferred_element_type=jnp.float32)
    adapter_bwd = jnp.einsum("snr,srd->snd", up_grad, down_sel, preferred_element_type=jnp.float32)
    back_send = jnp.concatenate(
        [adapter_bwd.astype(jnp.bfloat16), adapter_out.astype(jnp.bfloat16)], axis=2
    )
    back = lax.all_to_all(back_send, "dx", split_axis=0, concat_axis=0, tiled=True)

    def by_panel(small):
        small_p = jnp.take(small, panel_slot.reshape(-1), axis=0, mode="clip").reshape(
            column, n_x, blk, rank
        )
        small_p = jnp.where(panel_used[:, :, None, None], small_p, jnp.zeros_like(small_p))
        return small_p.reshape(column, n_x * blk, rank)

    rows_p = jnp.take(recv, panel_slot.reshape(-1), axis=0, mode="clip").reshape(
        column, n_x * blk, width_loc + out_loc
    )
    grad_up = jnp.einsum(
        "pnr,pnd->prd", by_panel(up_grad), rows_p, preferred_element_type=jnp.float32
    )
    grad_low = jnp.einsum(
        "pnr,pnd->prd", by_panel(down_low), rows_p, preferred_element_type=jnp.float32
    )
    feature = jnp.arange(width_loc + out_loc, dtype=jnp.int32)[None, None, :]
    grads_col = jnp.where(feature < width_loc, grad_up, grad_low)
    grads = lax.psum_scatter(
        grads_col.astype(jnp.bfloat16).reshape(column * rank, width_loc + out_loc),
        "dz",
        scatter_dimension=0,
        tiled=True,
    )
    grad_a = grads[:, :width_loc]
    grad_b = grads[:, width_loc:]
    grad_a = grad_a.astype(jnp.bfloat16).reshape(stored, rank, width_loc)
    grad_b = grad_b.astype(jnp.bfloat16).reshape(stored, rank, out_loc)
    base_bwd = jnp.einsum(
        "krc,dkc->rd",
        cot_parts,
        value_weight.reshape(width_loc, n_mp, out_loc),
        preferred_element_type=jnp.float32,
    )
    base_bwd = lax.optimization_barrier(base_bwd)
    mine_back = jnp.take(back, position, axis=0, mode="clip").reshape(rows, width_loc + out_loc)
    values = (base_t.T + mine_back[:, width_loc:].astype(jnp.float32)).astype(jnp.bfloat16)
    token_gradient = (base_bwd + mine_back[:, :width_loc].astype(jnp.float32)).astype(jnp.bfloat16)
    return (values, token_gradient, grad_a, grad_b)


def split_dp(mesh):
    devices = np.asarray(mesh.devices)
    n_dp, n_mp = devices.shape
    try:
        n_x = len({tuple(d.coords)[0] for d in devices[:, 0]})
    except (AttributeError, TypeError):
        n_x = 1
    if n_x < 1 or n_dp % n_x:
        n_x = 1
    return Mesh(devices.reshape(n_dp // n_x, n_x, n_mp), ("dz", "dx", "mp"))


def solution(mesh):
    in_specs = (
        P(DP, "mp"),
        P("mp", None),
        P(DP, None, "mp"),
        P(DP, None, "mp"),
        P(DP, "mp"),
        P(DP),
        P(DP),
        P(),
    )
    out_specs = (P(DP, "mp"), P(DP, "mp"), P(DP, None, "mp"), P(DP, None, "mp"))
    return jax.shard_map(
        shards, mesh=split_dp(mesh), in_specs=in_specs, out_specs=out_specs, check_vma=False
    )
```

profile of v0, /device:TPU:224, one launch (start us, length us, event | category | flops | bytes accessed | tf_op | source)
XLA Modules:
  0.0 285.4 jit_solution(7799087887903923186)
XLA Ops:
  7.2 2.0 pad_maximum_fusion.3
  9.3 0.7 all-gather.7.cloned.1.call-update
  10.0 0.7 pad_clamp_fusion.5
  10.7 1.4 gather_fusion
  12.0 1.4 gather_fusion.1
  13.4 6.0 %fusion.27 = f32[1024,1024]{1,0:T(8,128)} fusion(bf16[1024,1024]{1,0:T(8,128)(2,1)} %param.9, bf16[1024,1024]{1,0:T(8,128)(2,1)S(1)} %copy-done), kind=kOutput, calls=%fused_computation.109 | convolution fusion | flops 2147483648 | bytes 8388608 | tf_op jit(solution)/shard_map/dot_general | solution.py:49
  19.4 0.2 convert_reduce_fusion.1
  19.6 0.1 select_reduce_fusion.1
  19.7 0.6 copy-done.2
  20.3 0.7 gather_fusion.3
  21.0 2.8 gather_fusion.2
  23.8 4.9 %pad_maximum_fusion = bf16[64,32,1152]{2,1,0:T(8,128)(2,1)} fusion(bf16[64,32,128]{2,1,0:T(8,128)(2,1)S(1)} %gather_fusion.3, bf16[64,32,1024]{2,1,0:T(8,128)(2,1)} %gather_fusion.2), kind=kLoop, calls=%fused_computation.11 | loop fusion | flops 9437184 | bytes 9437184 | tf_op jit(solution)/shard_map/concatenate | solution.py:92
  28.8 5.1 %all-to-all-start = ((bf16[64,32,1152]{2,1,0:T(8,128)(2,1)}), bf16[64,32,1152]{2,1,0:T(8,128)(2,1)}, u32[]{:S(2)}, u32[]{:S(2)}) async-start(bf16[64,32,1152]{2,1,0:T(8,128)(2,1)} %pad_maximum_fusion), calls=%async_computation.1 | async-start | bytes 9437184 | tf_op jit(solution)/shard_map/all_to_all | solution.py:99
  33.9 0.6 dynamic-slice
  35.2 0.2 dynamic-update-slice
  35.4 55.9 %all-reduce = s32[128]{0:T(128)S(1)} all-reduce(s32[128]{0:T(128)S(1)} %dynamic-update-slice), channel_id=2, replica_groups=mesh['dz'=8,'dx'=4,'mp'=8] {'dx'}, use_global_device_ids=true, to_apply=%add | all-reduce | flops 128 | bytes 1024
  91.7 0.2 convert_reduce_fusion
  91.9 0.4 select_reduce_fusion.2
  92.3 0.1 copy.47
  92.4 0.1 copy.48
  92.5 0.1 copy.49
  92.6 0.1 copy.50
  92.7 0.1 copy.51
  92.8 0.1 copy.52
  92.8 0.1 copy.53
  92.9 0.1 copy.54
  93.0 0.1 copy.55
  93.1 0.1 copy.56
  93.2 0.1 copy.57
  93.3 0.1 copy.58
  93.4 0.1 copy.59
  93.8 0.1 stack.76
  94.0 0.1 select_reduce_fusion
  94.2 0.1 reshape.313
  94.3 0.1 copy.65
  94.7 8.8 %gather_fusion.8 = bf16[96,32,1152]{2,1,0:T(8,128)(2,1)} fusion(bf16[64,32,1152]{2,1,0:T(8,128)(2,1)} %all-to-all-done, s32[1024]{0:T(1024)S(1)} %pad_clamp_fusion), kind=kCustom, calls=%fused_computation.8 | custom fusion | bytes 14156160 | tf_op jit(solution)/shard_map/jit(_take)/gather | solution.py:125
  103.5 1.0 slice.63
  104.5 0.7 gather_fusion.5
  105.3 4.1 %slice.61 = bf16[24,64,1024]{2,1,0:T(8,128)(2,1)} slice(bf16[24,64,1152]{2,1,0:T(8,128)(2,1)} %all-gather.5.cloned.1.call-done), slice={[0:24], [0:64], [0:1024]} | slice | bytes 6291456 | tf_op jit(solution)/shard_map/slice | solution.py:87
  109.4 7.5 %gather_fusion.4 = bf16[64,64,1024]{2,1,0:T(8,128)(2,1)} fusion(bf16[24,64,1024]{2,1,0:T(8,128)(2,1)} %slice.61, s32[1024]{0:T(1024)S(1)} %pad_clamp_fusion.2), kind=kCustom, calls=%fused_computation.4 | custom fusion | bytes 16777472 | tf_op jit(solution)/shard_map/jit(_take)/gather | solution.py:103
  116.9 1.7 convolution_bitcast_fusion.1
  118.6 7.1 %fusion.4 = f32[1,64,32,64]{3,2,1,0:T(8,128)S(1)} fusion(bf16[64,64,1024]{2,1,0:T(8,128)(2,1)} %gather_fusion.4, bf16[64,32,1152]{2,1,0:T(8,128)(2,1)} %all-to-all-done), kind=kOutput, calls=%fused_computation.21 | convolution fusion | flops 268435456 | bytes 13107200 | tf_op jit(solution)/shard_map/snd,srd->snr/dot_general | solution.py:105
  125.7 1.6 pad_maximum_fusion.2
  127.3 53.8 %all-reduce.2 = bf16[2,64,32,64]{3,2,1,0:T(8,128)(2,1)S(1)} all-reduce(f32[2,64,32,64]{3,2,1,0:T(8,128)} %pad_maximum_fusion.2), channel_id=1, replica_groups=mesh['dz'=8,'dx'=4,'mp'=8] {'mp'}, use_global_device_ids=true, to_apply=%region_20.21 | all-reduce | flops 262144 | bytes 1572864 | tf_op jit(solution)/shard_map/psum | solution.py:107
  181.2 1.6 gather_fusion.7
  182.8 2.1 copy.67
  184.9 0.7 gather_fusion.9
  185.6 0.3 copy.68
  185.9 4.3 %fusion.10 = bf16[24,64,1152]{2,1,0:T(8,128)(2,1)S(1)} fusion(bf16[24,128,1152]{2,1,0:T(8,128)(2,1)} %bitcast.76, bf16[24,128,64]{1,2,0:T(8,128)(2,1)} %copy.67, pred[24,128]{1,0:T(8,128)(4,1)S(1)} %broadcast_in_dim.118), kind=kOutput, calls=%fused_computation.31 | convolution fusion | flops 453181440 | bytes 11013120 | tf_op jit(solution)/shard_map/pnr,pnd->prd/dot_general | solution.py:128
  190.3 6.2 %select_convert_fusion = bf16[24,64,1152]{2,1,0:T(8,128)(2,1)} fusion(bf16[24,64,1152]{2,1,0:T(8,128)(2,1)S(1)} %fusion.10, bf16[24,128,1152]{2,1,0:T(8,128)(2,1)} %bitcast.77, pred[1152]{0:T(1024)(128)(4,1)S(1)} %iota_compare_fusion.3, bf16[24,128,64]{1,2,0:T(8,128)(2,1)S(1)} %copy.68, pred[24,128]{1,0:T(8,128)(4,1)S(1)} %broadcast_in_dim.118), kind=kOutput, calls=%fused_computation.10 | convolution fusion | flops 454950912 | bytes 14553216 | tf_op jit(solution)/shard_map/pnr,pnd->prd/dot_general | solution.py:131
  196.5 0.4 convolution_convert_fusion.1
  196.9 4.6 %convolution_convert_fusion = bf16[64,32,1024]{2,1,0:T(8,128)(2,1)S(1)} fusion(bf16[64,64,1024]{2,1,0:T(8,128)(2,1)} %gather_fusion.4, bf16[2,64,32,64]{3,2,1,0:T(8,128)(2,1)S(1)} %all-reduce.2), kind=kOutput, calls=%fused_computation.16 | convolution fusion | flops 270532608 | bytes 13107200 | tf_op jit(solution)/shard_map/snr,srd->snd/dot_general | solution.py:112
  201.5 2.8 pad_maximum_fusion.1
  204.3 4.9 %all-to-all-start.1 = ((bf16[64,32,1152]{2,1,0:T(8,128)(2,1)}), bf16[64,32,1152]{2,1,0:T(8,128)(2,1)}, u32[]{:S(2)}, u32[]{:S(2)}) async-start(bf16[64,32,1152]{2,1,0:T(8,128)(2,1)} %pad_maximum_fusion.1), calls=%async_computation.2 | async-start | bytes 9437184 | tf_op jit(solution)/shard_map/all_to_all | solution.py:116
  209.3 6.7 %convolution_bitcast_fusion = f32[1024,1024]{1,0:T(8,128)} fusion(bf16[8,1024,128]{2,1,0:T(8,128)(2,1)} %bitcast.102, bf16[1024,1024]{1,0:T(8,128)(2,1)} %param.9), kind=kOutput, calls=%fused_computation.17 | convolution fusion | flops 2147483648 | bytes 8388608 | tf_op jit(solution)/shard_map/krc,dkc->rd/dot_general | solution.py:146
  216.0 47.0 %all-to-all-done.1 = bf16[64,32,1152]{2,1,0:T(8,128)(2,1)} async-done(((bf16[64,32,1152]{2,1,0:T(8,128)(2,1)}), bf16[64,32,1152]{2,1,0:T(8,128)(2,1)}, u32[]{:S(2)}, u32[]{:S(2)}) %all-to-all-start.1) | async-done | bytes 4718624 | tf_op jit(solution)/shard_map/all_to_all | solution.py:116
  263.0 4.6 %gather_fusion.6 = bf16[32,32,1152]{2,1,0:T(8,128)(2,1)} fusion(bf16[64,32,1152]{2,1,0:T(8,128)(2,1)} %all-to-all-done.1, s32[1024]{0:T(1024)S(1)} %pad_clamp_fusion.1), kind=kCustom, calls=%fused_computation.6 | custom fusion | bytes 4718720 | tf_op jit(solution)/shard_map/jit(_take)/gather | solution.py:153
  267.6 1.0 slice.66
  268.6 0.1 copy.70
  268.8 1.1 fusion.8
  269.9 0.8 copy.69
  270.7 5.0 %add_convert_fusion = bf16[1024,1024]{1,0:T(8,128)(2,1)} fusion(f32[1024,1024]{1,0:T(8,128)} %convolution_bitcast_fusion, bf16[1024,1152]{1,0:T(8,128)(2,1)} %bitcast.80), kind=kLoop, calls=%fused_computation.15 | loop fusion | flops 3145728 | bytes 8388608 | tf_op jit(solution)/shard_map/convert_element_type | solution.py:155
  275.7 1.8 slice.68
  277.5 1.4 slice.69
  (48 shorter events, 1.4 us)
Async XLA Ops:
  7.2 6.2 %copy-start = (bf16[1024,1024]{1,0:T(8,128)(2,1)S(1)}, bf16[1024,1024]{1,0:T(8,128)(2,1)}, u32[]{:S(2)}) copy-start(bf16[1024,1024]{1,0:T(8,128)(2,1)} %param.8) | copy-start | bytes 6291460
  7.2 96.3 %all-gather.5.cloned.1.call-start = ((), (), s32[]{:S(2)}) async-start(), calls=%async_computation.5 | async-start | bytes 3981312 | tf_op jit(solution)/shard_map/all_gather | solution.py:84
  9.2 200.1 %all-gather.7.cloned.1.call-start = ((), (), s32[]{:S(2)}) async-start(), calls=%async_computation.7 | async-start | bytes 2359296 | tf_op jit(solution)/shard_map/all_gather | solution.py:108
  10.0 258.8 %reduce-scatter.3.cloned.1.call-start = ((), (), s32[]{:S(2)}) async-start(), calls=%async_computation.4 | async-start | bytes 4718592 | tf_op jit(solution)/shard_map/reduce_scatter | solution.py:53
  19.4 0.9 copy-start.2
  28.8 5.2 %copy-start.3 = (u32[256]{0:T(256)S(1)}, u32[256]{0:T(256)}, u32[]{:S(2)}) copy-start(u32[256]{0:T(256)} %constant.110) | copy-start | bytes 3076
  28.8 65.9 %all-to-all-start = ((bf16[64,32,1152]{2,1,0:T(8,128)(2,1)}), bf16[64,32,1152]{2,1,0:T(8,128)(2,1)}, u32[]{:S(2)}, u32[]{:S(2)}) async-start(bf16[64,32,1152]{2,1,0:T(8,128)(2,1)} %pad_maximum_fusion), calls=%async_computation.1 | async-start | bytes 9437184 | tf_op jit(solution)/shard_map/all_to_all | solution.py:99
  33.9 241.8 %reduce-scatter.5.cloned.1.call-start = ((), (), s32[]{:S(2)}) async-start(), calls=%async_computation.6 | async-start | bytes 3981312 | tf_op jit(solution)/shard_map/reduce_scatter | solution.py:136
  204.3 58.7 %all-to-all-start.1 = ((bf16[64,32,1152]{2,1,0:T(8,128)(2,1)}), bf16[64,32,1152]{2,1,0:T(8,128)(2,1)}, u32[]{:S(2)}, u32[]{:S(2)}) async-start(bf16[64,32,1152]{2,1,0:T(8,128)(2,1)} %pad_maximum_fusion.1), calls=%async_computation.2 | async-start | bytes 9437184 | tf_op jit(solution)/shard_map/all_to_all | solution.py:116
  269.9 9.0 %copy-start.1 = (bf16[1024,1024]{1,0:T(8,128)(2,1)S(1)}, bf16[1024,1024]{1,0:T(8,128)(2,1)}, u32[]{:S(2)}) copy-start(bf16[1024,1024]{1,0:T(8,128)(2,1)} %param.8) | copy-start | bytes 6291460
Sparse Core Ops, SparseCore 0:
  10.4 47.1 all-gather.4
  59.4 28.2 all-gather.6
  90.3 40.7 reduce-scatter.2
  196.6 44.5 reduce-scatter.4
where the time goes:
time: 286 us; the launch traced here: 285 us
  blocking collectives  110 us (38%)
  waiting for transfers between devices  47.8 us (17%)
  local copies, waits for them, and re-layouts  46.8 us (16%)
  matrix products  37 us (13%)
  other arithmetic  19.2 us (7%)
  between operations  14.7 us (5%)
  starting transfers between devices  10.2 us (4%)
    unnamed x1, blocking collectives  55.9 us
    psum x1, blocking collectives, shards(): both = lax.psum(jnp.stack([down_part, up_part]), 'mp').astype(jnp.bfloat16)  53.8 us
    all_to_all x1, waiting for transfers between devices, shards(): lax.all_to_all(back_send, 'dx', split_axis=0, concat_axis=0, tiled=True)  47 us
    gather x1, local copies, waits for them, and re-layouts, shards(): jnp.take(recv, panel_slot.reshape(-1), axis=0, mode='clip')  8.82 us
    gather x1, local copies, waits for them, and re-layouts, shards(): down_sel = jnp.take(down_col, panel_at, axis=0, mode='clip')  7.48 us
    dot_general x1, matrix products, shards(): jnp.einsum('snd,srd->snr', tok_recv, down_sel, preferred_element_type=jnp...  7.12 us
    dot_general x1, matrix products, shards(): jnp.einsum('krc,dkc->rd', cot_parts, value_weight.reshape(width_loc, n_mp...  6.7 us
    dot_general x1, matrix products, shards(): jnp.einsum('pnr,pnd->prd', by_panel(down_low), rows_p, preferred_element_...  6.16 us
  transfers between devices with their start and end apart: 6, of which 1 were waited for; matrix products, arithmetic and copies ran while one was open for 34% of the time, Pallas kernels for 0%

commit v1 on v0

--- a/solution.py
+++ b/solution.py
@@ -104,7 +104,9 @@
     up_sel = jnp.take(up_col, panel_at, axis=0, mode="clip")
     down_part = jnp.einsum("snd,srd->snr", tok_recv, down_sel, preferred_element_type=jnp.float32)
     up_part = jnp.einsum("snc,src->snr", cot_recv, up_sel, preferred_element_type=jnp.float32)
-    both = lax.psum(jnp.stack([down_part, up_part]), "mp").astype(jnp.bfloat16)
+    both = jnp.sum(lax.all_gather(jnp.stack([down_part, up_part]), "mp"), axis=0).astype(
+        jnp.bfloat16
+    )
     cot_parts = lax.all_gather(cotangent, "mp", axis=0, tiled=False)
     down_low = both[0]
     up_grad = both[1]

time: 286 us -> 335 us (1.17); the launches traced: 285 us -> 329 us
  waiting for transfers between devices: 47.8 us -> 142 us
  blocking collectives: 110 us -> 50 us
  other arithmetic: 19.2 us -> 27.7 us
    all_gather x0 -> x1, waiting for transfers between devices: none -> 74.8 us  [shards(): lax.all_gather(jnp.stack([down_part, up_part]), 'mp')]
    psum x1 -> x0, blocking collectives: 53.8 us -> none  [shards(): both = lax.psum(jnp.stack([down_part, up_part]), 'mp').astype(jnp.bfloat16)]
    reduce_scatter x1, waiting for transfers between devices: 0.01 us -> 17.6 us  [shards(): lax.psum_scatter(grads_col.astype(jnp.bfloat16).reshape(column * rank, wi...]
    reduce_sum x0 -> x1, other arithmetic: none -> 8.37 us  [shards(): jnp.sum(lax.all_gather(jnp.stack([down_part, up_part]), 'mp'), axis=0)]
    unnamed x1, blocking collectives: 55.9 us -> 50 us
  transfers between devices with their start and end apart: 6 -> 7, of which waited for: 1 -> 3; matrix products, arithmetic and copies ran while one was open for 34% -> 29% of each run, Pallas kernels for 0% -> 0%
where the time goes in v1:
time: 335 us; the launch traced here: 329 us
  waiting for transfers between devices  142 us (42%)
  blocking collectives  50 us (15%)
  local copies, waits for them, and re-layouts  46.9 us (14%)
  matrix products  37.2 us (11%)
  other arithmetic  27.7 us (8%)
  between operations  14.7 us (4%)
  starting transfers between devices  10.5 us (3%)
    all_gather x1, waiting for transfers between devices, shards(): lax.all_gather(jnp.stack([down_part, up_part]), 'mp')  74.8 us
    unnamed x1, blocking collectives  50 us
    all_to_all x1, waiting for transfers between devices, shards(): lax.all_to_all(back_send, 'dx', split_axis=0, concat_axis=0, tiled=True)  48.2 us
    reduce_scatter x1, waiting for transfers between devices, shards(): lax.psum_scatter(grads_col.astype(jnp.bfloat16).reshape(column * rank, wi...  17.6 us
    gather x1, local copies, waits for them, and re-layouts, shards(): jnp.take(recv, panel_slot.reshape(-1), axis=0, mode='clip')  8.92 us
    reduce_sum x1, other arithmetic, shards(): jnp.sum(lax.all_gather(jnp.stack([down_part, up_part]), 'mp'), axis=0)  8.37 us
    gather x1, local copies, waits for them, and re-layouts, shards(): down_sel = jnp.take(down_col, panel_at, axis=0, mode='clip')  7.28 us
    dot_general x1, matrix products, shards(): jnp.einsum('snd,srd->snr', tok_recv, down_sel, preferred_element_type=jnp...  6.97 us
  transfers between devices with their start and end apart: 7, of which 3 were waited for; matrix products, arithmetic and copies ran while one was open for 29% of the time, Pallas kernels for 0%

profile of v1, /device:TPU:224, one launch (start us, length us, event | category | flops | bytes accessed | tf_op | source)
XLA Modules:
  0.0 328.9 jit_solution(1847602955891012609)
XLA Ops:
  7.2 2.0 pad_maximum_fusion.3
  9.2 0.7 pad_clamp_fusion.5
  9.9 1.4 gather_fusion
  11.2 1.4 gather_fusion.1
  12.6 0.2 convert_reduce_fusion.1
  12.9 1.6 gather_fusion.3
  14.5 2.7 gather_fusion.2
  17.3 5.0 %pad_maximum_fusion = bf16[64,32,1152]{2,1,0:T(8,128)(2,1)} fusion(bf16[64,32,128]{2,1,0:T(8,128)(2,1)S(1)} %gather_fusion.3, bf16[64,32,1024]{2,1,0:T(8,128)(2,1)} %gather_fusion.2), kind=kLoop, calls=%fused_computation.11 | loop fusion | flops 9437184 | bytes 9437184 | tf_op jit(solution)/shard_map/concatenate | solution.py:92
  22.2 5.0 %all-to-all-start = ((bf16[64,32,1152]{2,1,0:T(8,128)(2,1)}), bf16[64,32,1152]{2,1,0:T(8,128)(2,1)}, u32[]{:S(2)}, u32[]{:S(2)}) async-start(bf16[64,32,1152]{2,1,0:T(8,128)(2,1)} %pad_maximum_fusion), calls=%async_computation.1 | async-start | bytes 9437184 | tf_op jit(solution)/shard_map/all_to_all | solution.py:99
  27.3 5.9 %fusion.27 = f32[1024,1024]{1,0:T(8,128)} fusion(bf16[1024,1024]{1,0:T(8,128)(2,1)} %param.9, bf16[1024,1024]{1,0:T(8,128)(2,1)S(1)} %copy-done), kind=kOutput, calls=%fused_computation.109 | convolution fusion | flops 2147483648 | bytes 8388608 | tf_op jit(solution)/shard_map/dot_general | solution.py:49
  33.2 0.6 dynamic-slice
  34.5 0.2 dynamic-update-slice
  34.7 50.0 %all-reduce = s32[128]{0:T(128)S(1)} all-reduce(s32[128]{0:T(128)S(1)} %dynamic-update-slice), channel_id=2, replica_groups=mesh['dz'=8,'dx'=4,'mp'=8] {'dx'}, use_global_device_ids=true, to_apply=%add | all-reduce | flops 128 | bytes 1024
  85.0 0.2 convert_reduce_fusion
  85.2 0.4 select_reduce_fusion.2
  85.6 0.1 copy.47
  85.7 0.1 copy.48
  85.8 0.1 copy.49
  85.9 0.1 copy.50
  86.0 0.1 copy.51
  86.1 0.1 copy.52
  86.2 0.1 copy.53
  86.3 0.1 copy.54
  86.4 0.1 copy.55
  86.6 0.1 copy.57
  86.7 0.1 copy.59
  87.1 0.1 stack.76
  87.4 1.0 slice.63
  88.4 0.7 gather_fusion.5
  89.1 4.0 %slice.61 = bf16[24,64,1024]{2,1,0:T(8,128)(2,1)} slice(bf16[24,64,1152]{2,1,0:T(8,128)(2,1)} %all-gather.7.cloned.1.call-done), slice={[0:24], [0:64], [0:1024]} | slice | bytes 6291456 | tf_op jit(solution)/shard_map/slice | solution.py:87
  93.2 7.3 %gather_fusion.4 = bf16[64,64,1024]{2,1,0:T(8,128)(2,1)} fusion(bf16[24,64,1024]{2,1,0:T(8,128)(2,1)} %slice.61, s32[1024]{0:T(1024)S(1)} %pad_clamp_fusion.2), kind=kCustom, calls=%fused_computation.4 | custom fusion | bytes 16777472 | tf_op jit(solution)/shard_map/jit(_take)/gather | solution.py:103
  100.5 1.7 convolution_bitcast_fusion.1
  102.1 7.0 %fusion.4 = f32[1,64,32,64]{3,2,1,0:T(8,128)S(1)} fusion(bf16[64,64,1024]{2,1,0:T(8,128)(2,1)} %gather_fusion.4, bf16[64,32,1152]{2,1,0:T(8,128)(2,1)} %all-to-all-done), kind=kOutput, calls=%fused_computation.21 | convolution fusion | flops 268435456 | bytes 13107200 | tf_op jit(solution)/shard_map/snd,srd->snr/dot_general | solution.py:105
  109.1 1.6 pad_maximum_fusion.2
  110.8 0.7 all-gather.11.cloned.1.call-update
  111.5 0.5 reduce-scatter.3.cloned.1.call-update
  112.0 0.2 reduce-scatter.5.cloned.1.call-start
  112.3 0.1 select_reduce_fusion
  112.5 0.1 reshape.313
  112.6 0.1 copy.65
  112.9 8.9 %gather_fusion.8 = bf16[96,32,1152]{2,1,0:T(8,128)(2,1)} fusion(bf16[64,32,1152]{2,1,0:T(8,128)(2,1)} %all-to-all-done, s32[1024]{0:T(1024)S(1)} %pad_clamp_fusion), kind=kCustom, calls=%fused_computation.8 | custom fusion | bytes 14156160 | tf_op jit(solution)/shard_map/jit(_take)/gather | solution.py:127
  121.9 74.8 %all-gather.9.cloned.1.call-done = f32[16,64,32,64]{3,2,1,0:T(8,128)} async-done(((f32[2,64,32,64]{3,2,1,0:T(8,128)}), f32[16,64,32,64]{3,2,1,0:T(8,128)}) %all-gather.9.cloned.1.call-update) | async-done | bytes 8388624 | tf_op jit(solution)/shard_map/all_gather | solution.py:107
  196.7 8.4 %reduce_sum.210 = bf16[2,64,32,64]{3,2,1,0:T(8,128)(2,1)S(1)} reduce(f32[8,2,64,32,64]{4,3,2,1,0:T(8,128)} %bitcast.79, f32[]{:T(128)} %constant.105.clone.1), dimensions={0}, to_apply=%region_20.21 | reduce | flops 1835008 | bytes 8912900 | tf_op jit(solution)/shard_map/reduce_sum | solution.py:107
  205.1 1.6 gather_fusion.7
  206.7 2.1 copy.67
  208.8 0.7 gather_fusion.9
  209.6 0.3 copy.68
  209.9 4.6 %fusion.10 = bf16[24,64,1152]{2,1,0:T(8,128)(2,1)S(1)} fusion(bf16[24,128,1152]{2,1,0:T(8,128)(2,1)} %bitcast.77, bf16[24,128,64]{1,2,0:T(8,128)(2,1)} %copy.67, pred[24,128]{1,0:T(8,128)(4,1)S(1)} %broadcast_in_dim.118), kind=kOutput, calls=%fused_computation.31 | convolution fusion | flops 453181440 | bytes 11013120 | tf_op jit(solution)/shard_map/pnr,pnd->prd/dot_general | solution.py:130
  214.5 6.2 %select_convert_fusion = bf16[24,64,1152]{2,1,0:T(8,128)(2,1)} fusion(bf16[24,64,1152]{2,1,0:T(8,128)(2,1)S(1)} %fusion.10, bf16[24,128,1152]{2,1,0:T(8,128)(2,1)} %bitcast.78, pred[1152]{0:T(1024)(128)(4,1)S(1)} %iota_compare_fusion.3, bf16[24,128,64]{1,2,0:T(8,128)(2,1)S(1)} %copy.68, pred[24,128]{1,0:T(8,128)(4,1)S(1)} %broadcast_in_dim.118), kind=kOutput, calls=%fused_computation.10 | convolution fusion | flops 454950912 | bytes 14553216 | tf_op jit(solution)/shard_map/pnr,pnd->prd/dot_general | solution.py:133
  220.7 0.4 convolution_convert_fusion.1
  221.1 4.7 %convolution_convert_fusion = bf16[64,32,1024]{2,1,0:T(8,128)(2,1)S(1)} fusion(bf16[64,64,1024]{2,1,0:T(8,128)(2,1)} %gather_fusion.4, bf16[2,64,32,64]{3,2,1,0:T(8,128)(2,1)S(1)} %reduce_sum.210), kind=kOutput, calls=%fused_computation.16 | convolution fusion | flops 270532608 | bytes 13107200 | tf_op jit(solution)/shard_map/snr,srd->snd/dot_general | solution.py:114
  225.9 2.8 pad_maximum_fusion.1
  228.7 5.2 %all-to-all-start.1 = ((bf16[64,32,1152]{2,1,0:T(8,128)(2,1)}), bf16[64,32,1152]{2,1,0:T(8,128)(2,1)}, u32[]{:S(2)}, u32[]{:S(2)}) async-start(bf16[64,32,1152]{2,1,0:T(8,128)(2,1)} %pad_maximum_fusion.1), calls=%async_computation.2 | async-start | bytes 9437184 | tf_op jit(solution)/shard_map/all_to_all | solution.py:118
  233.9 6.7 %convolution_bitcast_fusion = f32[1024,1024]{1,0:T(8,128)} fusion(bf16[8,1024,128]{2,1,0:T(8,128)(2,1)} %bitcast.104, bf16[1024,1024]{1,0:T(8,128)(2,1)} %param.9), kind=kOutput, calls=%fused_computation.17 | convolution fusion | flops 2147483648 | bytes 8388608 | tf_op jit(solution)/shard_map/krc,dkc->rd/dot_general | solution.py:148
  240.5 48.2 %all-to-all-done.1 = bf16[64,32,1152]{2,1,0:T(8,128)(2,1)} async-done(((bf16[64,32,1152]{2,1,0:T(8,128)(2,1)}), bf16[64,32,1152]{2,1,0:T(8,128)(2,1)}, u32[]{:S(2)}, u32[]{:S(2)}) %all-to-all-start.1) | async-done | bytes 4718624 | tf_op jit(solution)/shard_map/all_to_all | solution.py:118
  288.8 4.6 %gather_fusion.6 = bf16[32,32,1152]{2,1,0:T(8,128)(2,1)} fusion(bf16[64,32,1152]{2,1,0:T(8,128)(2,1)} %all-to-all-done.1, s32[1024]{0:T(1024)S(1)} %pad_clamp_fusion.1), kind=kCustom, calls=%fused_computation.6 | custom fusion | bytes 4718720 | tf_op jit(solution)/shard_map/jit(_take)/gather | solution.py:155
  293.4 1.0 slice.66
  294.4 0.1 copy.70
  294.5 1.1 fusion.8
  295.7 0.8 copy.69
  296.5 5.0 %add_convert_fusion = bf16[1024,1024]{1,0:T(8,128)(2,1)} fusion(f32[1024,1024]{1,0:T(8,128)} %convolution_bitcast_fusion, bf16[1024,1152]{1,0:T(8,128)(2,1)} %bitcast.82), kind=kLoop, calls=%fused_computation.15 | loop fusion | flops 3145728 | bytes 8388608 | tf_op jit(solution)/shard_map/convert_element_type | solution.py:157
  301.5 17.6 %reduce-scatter.5.cloned.1.call-done = bf16[192,1152]{1,0:T(8,128)(2,1)} async-done(((bf16[1536,1152]{1,0:T(8,128)(2,1)}), bf16[192,1152]{1,0:T(8,128)(2,1)}) %reduce-scatter.5.cloned.1.call-update) | async-done | bytes 442384 | tf_op jit(solution)/shard_map/reduce_scatter | solution.py:138
  319.2 1.8 slice.68
  320.9 1.4 slice.69
  (49 shorter events, 1.7 us)
Async XLA Ops:
  7.2 7.4 %copy-start = (bf16[1024,1024]{1,0:T(8,128)(2,1)S(1)}, bf16[1024,1024]{1,0:T(8,128)(2,1)}, u32[]{:S(2)}) copy-start(bf16[1024,1024]{1,0:T(8,128)(2,1)} %param.8) | copy-start | bytes 6291460
  7.2 80.2 %all-gather.7.cloned.1.call-start = ((), (), s32[]{:S(2)}) async-start(), calls=%async_computation.5 | async-start | bytes 3981312 | tf_op jit(solution)/shard_map/all_gather | solution.py:84
  22.2 78.2 %all-to-all-start = ((bf16[64,32,1152]{2,1,0:T(8,128)(2,1)}), bf16[64,32,1152]{2,1,0:T(8,128)(2,1)}, u32[]{:S(2)}, u32[]{:S(2)}) async-start(bf16[64,32,1152]{2,1,0:T(8,128)(2,1)} %pad_maximum_fusion), calls=%async_computation.1 | async-start | bytes 9437184 | tf_op jit(solution)/shard_map/all_to_all | solution.py:99
  27.2 169.5 %all-gather.9.cloned.1.call-start = ((), (), s32[]{:S(2)}) async-start(), calls=%async_computation.7 | async-start | bytes 18874368 | tf_op jit(solution)/shard_map/all_gather | solution.py:107
  27.3 6.0 %copy-start.2 = (u32[256]{0:T(256)S(1)}, u32[256]{0:T(256)}, u32[]{:S(2)}) copy-start(u32[256]{0:T(256)} %constant.112) | copy-start | bytes 3076
  110.7 123.2 %all-gather.11.cloned.1.call-start = ((), (), s32[]{:S(2)}) async-start(), calls=%async_computation.8 | async-start | bytes 2359296 | tf_op jit(solution)/shard_map/all_gather | solution.py:110
  111.5 183.1 %reduce-scatter.3.cloned.1.call-start = ((), (), s32[]{:S(2)}) async-start(), calls=%async_computation.4 | async-start | bytes 4718592 | tf_op jit(solution)/shard_map/reduce_scatter | solution.py:53
  112.0 207.1 %reduce-scatter.5.cloned.1.call-start = ((), (), s32[]{:S(2)}) async-start(), calls=%async_computation.6 | async-start | bytes 3981312 | tf_op jit(solution)/shard_map/reduce_scatter | solution.py:138
  228.7 60.1 %all-to-all-start.1 = ((bf16[64,32,1152]{2,1,0:T(8,128)(2,1)}), bf16[64,32,1152]{2,1,0:T(8,128)(2,1)}, u32[]{:S(2)}, u32[]{:S(2)}) async-start(bf16[64,32,1152]{2,1,0:T(8,128)(2,1)} %pad_maximum_fusion.1), calls=%async_computation.2 | async-start | bytes 9437184 | tf_op jit(solution)/shard_map/all_to_all | solution.py:118
  295.6 26.7 %copy-start.1 = (bf16[1024,1024]{1,0:T(8,128)(2,1)S(1)}, bf16[1024,1024]{1,0:T(8,128)(2,1)}, u32[]{:S(2)}) copy-start(bf16[1024,1024]{1,0:T(8,128)(2,1)} %param.8) | copy-start | bytes 6291460
Sparse Core Ops, SparseCore 0:
  10.4 47.1 all-gather.6
  110.8 85.7 all-gather.8
  198.5 28.3 all-gather.10
  229.3 41.5 reduce-scatter.2
  273.3 45.7 reduce-scatter.4
